TPU v7x, 32 devices: a whole 2x2x4 slice. The times are simulated.
32 devices in a mesh: kpt: 8 (over z, core), row: 4 (over y, x).
Axes of the slice: x: 2, y: 2, z: 4, core: 2. Of those that a mesh axis runs over, the one named last changes fastest.
Arguments:
- occ_orbitals: bfloat16 [32, 2048, 128], P('kpt', 'row'), may hold values from -0.5 to 0.5
- virt_orbitals: bfloat16 [32, 2048, 256], P('kpt', 'row'), may hold values from -0.375 to 0.375
- occ_gap: bfloat16 [32, 128], P('kpt'), may hold values from 0.049804688 to 3
- virt_gap: bfloat16 [32, 256], P('kpt'), may hold values from 0.049804688 to 3
- partner: int32 [3, 32], replicated, may hold values from 0 to 31, as said below
Outputs:
- chi: float32 [3, 4, 2048, 2048], P(None, None, 'row', 'kpt')
Inputs may be any that keep to these rules, and one draw needn't show every extreme that they name: For each transfer q there is a shift s_q of 0 to 4 with partner[q, k] = (k - s_q) mod 32 for every k; the shifts of different transfers differ, and some transfer has s_q = 4.
All inputs are finite; a program needn't handle non-finite values.
Results may differ from a plain program's by a relative error of at most 0.0003.
Values may be sent and summed in bfloat16 or wider, within the bound.
A program may use at most 384 MiB of HBM per device.

v0:
```python
import functools

import jax
import jax.numpy as jnp
from jax import lax
from jax.experimental import pallas as pl
from jax.experimental.pallas import tpu as pltpu
from jax.sharding import PartitionSpec as P

NTAU = 4
PAD = 16
SUB = 32
LAG = 1


def kernel(nk, nr, per, occ_ref, virt_ref, gap_ref, partner_ref, out_ref, rows, cols, og, vg, stage, out_sem,
           local_sem, row_recv, col_recv, right_send, left_send, sib_send, col_send):
    K = nk * per
    npts, nocc = occ_ref.shape[1], occ_ref.shape[2]
    nall = rows.shape[2]
    ncol = cols.shape[1]
    j = lax.axis_index("kpt")
    i = lax.axis_index("row")
    c, s = j // 2, j % 2
    nc = nk // 2
    cpr = nk // nr
    root = j // cpr
    off = pl.multiple_of((j % cpr) * ncol, ncol)
    transfers = partner_ref.shape[0]

    def place(index):
        return jnp.where(index % 2 == 0, index // 2, nr - 1 - index // 2)

    def at_place(p):
        return jnp.where(p < nr // 2, 2 * p, 2 * (nr - 1 - p) + 1)

    me, top = place(i), place(root)
    ahead, behind = at_place((me + 1) % nr), at_place((me + nr - 1) % nr)
    dist_a, dist_b = (me - top + nr) % nr, (top - me + nr) % nr
    is_root = i == root
    has_right, has_left = c + 1 < nc, c > 0

    locals_ = []
    for a in range(per):
        m = j * per + a
        locals_.append((
            pltpu.make_async_copy(occ_ref.at[a], rows.at[m, pl.ds(0, npts), pl.ds(0, nocc)], local_sem.at[a, 0]),
            pltpu.make_async_copy(virt_ref.at[a], rows.at[m, pl.ds(0, npts), pl.ds(nocc, nall - nocc)], local_sem.at[a, 1]),
            pltpu.make_async_copy(gap_ref.at[a], rows.at[m, pl.ds(npts, PAD)], local_sem.at[a, 2]),
        ))
    for group in locals_:
        for copy in group:
            copy.start()

    barrier = pltpu.get_barrier_semaphore()

    def greet(device):
        pl.semaphore_signal(barrier, inc=1, device_id=device, device_id_type=pl.DeviceIdType.MESH)

    greet((j + 1 - 2 * s, i))
    greet((j, ahead))
    greet((j, behind))

    @pl.when(has_right)
    def _():
        greet((j + 2, i))

    @pl.when(has_left)
    def _():
        greet((j - 2, i))

    pl.semaphore_wait(barrier, 3 + has_right.astype(jnp.int32) + has_left.astype(jnp.int32))

    for group in locals_:
        for copy in group:
            copy.wait()

    def remote(src, dst, send, recv, device):
        return pltpu.make_async_remote_copy(src_ref=src, dst_ref=dst, send_sem=send, recv_sem=recv,
                                            device_id=device, device_id_type=pl.DeviceIdType.MESH)

    def to_right(m):
        return remote(rows.at[m], rows.at[m], right_send.at[m], row_recv.at[m], (j + 2, i))

    def to_left(m):
        return remote(rows.at[m], rows.at[m], left_send.at[m], row_recv.at[m], (j - 2, i))

    def to_sib(m):
        return remote(rows.at[m], rows.at[m], sib_send.at[m], row_recv.at[m], (j + 1 - 2 * s, i))

    def col_copy(m, device, from_root):
        src = rows.at[m, pl.ds(off, ncol)] if from_root else cols.at[m]
        return remote(src, cols.at[m], col_send.at[m], col_recv.at[m], (j, device))

    def root_copy(m):
        return pltpu.make_async_copy(rows.at[m, pl.ds(off, ncol)], cols.at[m], col_recv.at[m])

    def wait_row(m):
        pltpu.make_async_copy(rows.at[m], rows.at[m], row_recv.at[m]).wait()

    def wait_col(m):
        pltpu.make_async_copy(cols.at[m], cols.at[m], col_recv.at[m]).wait()

    def way(m):
        return (m + m // per) % 2

    def root_send(m, start):
        @pl.when(is_root)
        def _():
            if start:
                root_copy(m).start()
            for parity, device in ((0, ahead), (1, behind)):
                @pl.when(way(m) == parity)
                def _():
                    copy = col_copy(m, device, True)
                    copy.start() if start else copy.wait_send()

    def row_stage(f, start):
        h, a = f // per, f % per

        def go(copy):
            copy.start() if start else copy.wait_send()

        @pl.when(h == 0)
        def _():
            m = j * per + a

            @pl.when(has_right)
            def _():
                go(to_right(m))

            @pl.when(has_left)
            def _():
                go(to_left(m))

            go(to_sib(m))
            root_send(m, start)

        for left in (True, False):
            there = (c - h >= 0) if left else (c + h < nc)
            src = (c - h) if left else (c + h)
            onward = has_right if left else has_left

            @pl.when(there & (h > 0))
            def _():
                m = (2 * src + s) * per + a
                if start:
                    wait_row(m)

                @pl.when(onward)
                def _():
                    go(to_right(m) if left else to_left(m))

                go(to_sib(m))
                root_send(m, start)

        for left in (True, False):
            there = (c - h >= 0) if left else ((c + h < nc) & (h > 0))
            src = (c - h) if left else (c + h)

            @pl.when(there)
            def _():
                m = (2 * src + 1 - s) * per + a
                if start:
                    wait_row(m)
                root_send(m, start)

    contract = (((1,), (1,)), ((), ()))

    def green(k, moment):
        gap = rows[k, pl.ds(npts, PAD), :].astype(jnp.float32)[0:1]
        factor = jnp.exp(-gap * moment)
        panel = (rows[k, pl.ds(0, npts), :].astype(jnp.float32) * factor).astype(jnp.bfloat16)
        column = cols[k]
        og[k] = lax.dot_general(panel[:, :nocc], column[:, :nocc], contract, preferred_element_type=jnp.float32)
        vg[k] = lax.dot_general(panel[:, nocc:], column[:, nocc:], contract, preferred_element_type=jnp.float32)

    def green_stage(f):
        h, a = f // per, f % per
        for left in (True, False):
            there = (c - h >= 0) if left else ((c + h < nc) & (h > 0))
            src = (c - h) if left else (c + h)

            @pl.when(there)
            def _():
                for core in range(2):
                    green((2 * src + core) * per + a, 0.25)

    def col_stage(f, start, parity, dist, device):
        h, a = f // per, f % per
        for left in (True, False):
            there = (c - h >= 0) if left else ((c + h < nc) & (h > 0))
            src = (c - h) if left else (c + h)
            for core in range(2):
                m = (2 * src + core) * per + a

                @pl.when(there & (way(m) == parity))
                def _():
                    if start:
                        wait_col(m)

                    @pl.when((dist > 0) & (dist < nr - 1))
                    def _():
                        copy = col_copy(m, device, False)
                        copy.start() if start else copy.wait_send()

    total = nc * per
    ways = ((0, dist_a, ahead), (1, dist_b, behind))

    def step(f, carry):
        @pl.when(f < total)
        def _():
            row_stage(f, True)

        for parity, dist, device in ways:
            then = f - LAG * jnp.maximum(dist, 1)

            @pl.when((then >= 0) & (then < total))
            def _():
                col_stage(then, True, parity, dist, device)

        ready = f - LAG * (nr - 1)

        @pl.when(ready >= 0)
        def _():
            green_stage(ready)

        return carry

    lax.fori_loop(0, total + LAG * (nr - 1), step, 0)

    def out_copy(t):
        return pltpu.make_async_copy(stage.at[t % 2], out_ref.at[:, t], out_sem.at[t % 2])

    def block(t, carry):
        @pl.when(t > 1)
        def _():
            out_copy(t - 2).wait()

        @pl.when(t > 0)
        def _():
            moment = jnp.where(t == 1, 0.5, jnp.where(t == 2, 1.0, 2.0)).astype(jnp.float32)

            def one(k, inner):
                green(k, moment)
                return inner

            lax.fori_loop(0, K, one, 0, unroll=8)

        def piece(p, inner):
            here = pl.ds(pl.multiple_of(p * SUB, SUB), SUB)

            def add(k, sums):
                occ = og[k, here, :]
                return tuple(x + occ * vg[partner_ref[q, k], here, :] for q, x in enumerate(sums))

            zero = jnp.zeros((SUB, ncol), jnp.float32)
            sums = lax.fori_loop(0, K, add, (zero,) * transfers, unroll=16)
            for q in range(transfers):
                stage[t % 2, q, here, :] = sums[q]
            return inner

        lax.fori_loop(0, npts // SUB, piece, 0)
        out_copy(t).start()
        return carry

    lax.fori_loop(0, NTAU, block, 0)
    for t in (NTAU - 2, NTAU - 1):
        out_copy(t).wait()

    def finish(f, carry):
        row_stage(f, False)
        for parity, dist, device in ways:
            col_stage(f, False, parity, dist, device)
        return carry

    lax.fori_loop(0, total, finish, 0)


def on_device(nk, nr, occ_orbitals, virt_orbitals, occ_gap, virt_gap, partner):
    per, npts, nocc = occ_orbitals.shape
    nv = virt_orbitals.shape[2]
    K, ncol, nall = nk * per, npts * nr // nk, nocc + nv
    tile = npts
    transfers = partner.shape[0]
    gaps = jnp.broadcast_to(jnp.concatenate([occ_gap, virt_gap], axis=1)[:, None, :], (per, PAD, nall))
    dma = pltpu.SemaphoreType.DMA
    return pl.pallas_call(
        functools.partial(kernel, nk, nr, per),
        out_shape=jax.ShapeDtypeStruct((transfers, NTAU, npts, ncol), jnp.float32),
        in_specs=[pl.BlockSpec(memory_space=pl.ANY)] * 3 + [pl.BlockSpec(memory_space=pltpu.SMEM)],
        out_specs=pl.BlockSpec(memory_space=pl.ANY),
        scratch_shapes=[
            pltpu.VMEM((K, npts + PAD, nall), jnp.bfloat16),
            pltpu.VMEM((K, ncol, nall), jnp.bfloat16),
            pltpu.VMEM((K, tile, ncol), jnp.float32),
            pltpu.VMEM((K, tile, ncol), jnp.float32),
            pltpu.VMEM((2, transfers, npts, ncol), jnp.float32), dma((2,)),
            dma((per, 3)), dma((K,)), dma((K,)), dma((K,)), dma((K,)), dma((K,)), dma((K,)),
        ],
        compiler_params=pltpu.CompilerParams(
            collective_id=0, has_side_effects=True, vmem_limit_bytes=62 * 2**20),
    )(occ_orbitals, virt_orbitals, gaps, partner)


def solution(mesh):
    in_specs = (P("kpt", "row", None), P("kpt", "row", None), P("kpt", None), P("kpt", None), P())
    out_specs = P(None, None, "row", "kpt")
    return jax.shard_map(
        functools.partial(on_device, mesh.shape["kpt"], mesh.shape["row"]),
        mesh=mesh, in_specs=in_specs, out_specs=out_specs, check_vma=False,
    )
```

profile of v0, /device:TPU:2, one launch (start us, length us, event | category | flops | bytes accessed | tf_op | source)
XLA Modules:
  0.0 169.8 jit_solution(15140478116457578544)
XLA Ops:
  0.0 0.7 pad_maximum_fusion
  0.7 0.6 broadcast_in_dim.2.gap_ref
  1.3 162.6 %shard_map.55 = f32[3,4,512,256]{3,2,1,0:T(8,128)} custom-call(bf16[4,512,128]{2,1,0:T(8,128)(2,1)} %occ_ref.1, bf16[4,512,256]{2,1,0:T(8,128)(2,1)} %virt_ref.1, bf16[4,16,384]{2,1,0:T(8,128)(2,1)} %broadcast_in_dim.2.gap_ref, s32[3,32]{1,0:T(4,128)} %partner_ref.1), custom_call_target="tpu_custom_call" | custom-call | tf_op jit(solution)/shard_map/pallas_call | solution.py:288
  163.9 5.9 %copy.7 = f32[3,4,512,256]{3,2,1,0:T(8,128)} copy(f32[3,4,512,256]{3,2,1,0:T(8,128)} %shard_map.55) | data formatting | bytes 12582912
where the time goes:
time: 172 us; the launch traced here: 170 us
  Pallas kernels  163 us (95%)
  local copies, waits for them, and re-layouts  6.52 us (4%)
    pallas_call x1, Pallas kernels, on_device(): pl.pallas_call(functools.partial(kernel, nk, nr, per), out_shape=jax.Shap...  163 us
    unnamed x1, local copies, waits for them, and re-layouts  5.89 us

commit v1 on v0

v1 whole, which is shorter than its diff:
```python
import functools

import jax
import jax.numpy as jnp
from jax import lax
from jax.experimental import pallas as pl
from jax.experimental.pallas import tpu as pltpu
from jax.sharding import PartitionSpec as P

NTAU = 4
PAD = 16
SUB = 32
PIECES = 4


def kernel(nk, nr, per, occ_ref, virt_ref, gap_ref, partner_ref, chi, rows, cols, gaps, og, vg, last_og, last_vg,
           local_sem, row_recv, flow_send, sib_send, gap_recv, gap_flow, gap_sib, col_recv, col_send):
    K = nk * per
    npts, nocc = occ_ref.shape[1], occ_ref.shape[2]
    nall = rows.shape[2]
    ncol = cols.shape[1]
    width = ncol // PIECES
    transfers = partner_ref.shape[0]
    j = lax.axis_index("kpt")
    i = lax.axis_index("row")
    c, s = j // 2, j % 2
    nc = nk // 2
    cpr = nk // nr
    root = j // cpr
    off = (j % cpr) * ncol
    span = 2 * per

    def place(index):
        return jnp.where(index % 2 == 0, index // 2, nr - 1 - index // 2)

    def at_place(p):
        return jnp.where(p < nr // 2, 2 * p, 2 * (nr - 1 - p) + 1)

    me, top = place(i), place(root)
    ahead, behind = at_place((me + 1) % nr), at_place((me + nr - 1) % nr)
    dist_a, dist_b = (me - top + nr) % nr, (top - me + nr) % nr
    is_root = i == root
    up = s == 0
    has_next = jnp.where(up, c + 1 < nc, c > 0)
    has_prev = jnp.where(up, c > 0, c + 1 < nc)
    sib = j + 1 - 2 * s
    onward = j + 2 - 4 * s
    before = j - 2 + 4 * s

    def local_rows(a):
        m = j * per + a
        return (pltpu.make_async_copy(occ_ref.at[a], rows.at[m, :, pl.ds(0, nocc)], local_sem.at[a, 0]),
                pltpu.make_async_copy(virt_ref.at[a], rows.at[m, :, pl.ds(nocc, nall - nocc)], local_sem.at[a, 1]))

    local_gap = pltpu.make_async_copy(gap_ref, gaps.at[j], gap_recv.at[j])
    local_gap.start()
    for a in range(per):
        for copy in local_rows(a):
            copy.start()

    barrier = pltpu.get_barrier_semaphore()

    def greet(device):
        pl.semaphore_signal(barrier, inc=1, device_id=device, device_id_type=pl.DeviceIdType.MESH)

    greet((sib, i))
    greet((j, ahead))
    greet((j, behind))

    @pl.when(has_next)
    def _():
        greet((onward, i))

    @pl.when(has_prev)
    def _():
        greet((before, i))

    pl.semaphore_wait(barrier, 3 + has_next.astype(jnp.int32) + has_prev.astype(jnp.int32))

    def remote(src, dst, send, recv, device):
        return pltpu.make_async_remote_copy(src_ref=src, dst_ref=dst, send_sem=send, recv_sem=recv,
                                            device_id=device, device_id_type=pl.DeviceIdType.MESH)

    def row_flow(m):
        return remote(rows.at[m], rows.at[m], flow_send.at[m], row_recv.at[m], (onward, i))

    def row_sib(m):
        return remote(rows.at[m], rows.at[m], sib_send.at[m], row_recv.at[m], (sib, i))

    def gap_on(b):
        return remote(gaps.at[b], gaps.at[b], gap_flow.at[b], gap_recv.at[b], (onward, i))

    def gap_over(b):
        return remote(gaps.at[b], gaps.at[b], gap_sib.at[b], gap_recv.at[b], (sib, i))

    def part(p):
        return pl.ds(p * width, width)

    def source(m, p):
        return rows.at[m, pl.ds(pl.multiple_of(off + p * width, width), width)]

    def col_copy(m, p, device, from_root):
        src = source(m, p) if from_root else cols.at[m, part(p)]
        return remote(src, cols.at[m, part(p)], col_send.at[m, p], col_recv.at[m, p], (j, device))

    def root_copy(m, p):
        return pltpu.make_async_copy(source(m, p), cols.at[m, part(p)], col_recv.at[m, p])

    def wait_row(m):
        pltpu.make_async_copy(rows.at[m], rows.at[m], row_recv.at[m]).wait()

    def wait_gap(b):
        pltpu.make_async_copy(gaps.at[b], gaps.at[b], gap_recv.at[b]).wait()

    def wait_col(m, p):
        pltpu.make_async_copy(cols.at[m, part(p)], cols.at[m, part(p)], col_recv.at[m, p]).wait()

    ways = tuple((p, (dist_a, dist_b)[p % 2], (ahead, behind)[p % 2]) for p in range(PIECES))

    def root_send(m, start):
        @pl.when(is_root)
        def _():
            for p, _, device in ways:
                copy = col_copy(m, p, device, True)
                copy.start() if start else copy.wait_send()
                if start:
                    root_copy(m, p).start()

    def arrivals(n):
        h, idx = n // span, n % span
        low, high = c - h, c + h
        first = low * span + idx
        second = high * span + (idx + per) % span
        flow_ok = jnp.where(up, low >= 0, high < nc)
        other_ok = (h > 0) & jnp.where(up, high < nc, low >= 0)
        return h, idx, jnp.where(up, first, second), flow_ok, jnp.where(up, second, first), other_ok

    def row_stage(n, start):
        h, idx, fm, flow_ok, om, other_ok = arrivals(n)
        own = (h == 0) & (idx < per)
        lead = idx % per == 0

        def go(copy):
            copy.start() if start else copy.wait_send()

        @pl.when(flow_ok)
        def _():
            if start:
                @pl.when(own)
                def _():
                    for copy in local_rows(idx % per):
                        copy.wait()

                @pl.when(jnp.logical_not(own))
                def _():
                    wait_row(fm)

                @pl.when(lead)
                def _():
                    wait_gap(fm // per)

            @pl.when(has_next)
            def _():
                go(row_flow(fm))

                @pl.when(lead)
                def _():
                    go(gap_on(fm // per))

            @pl.when((h > 0) | own)
            def _():
                go(row_sib(fm))

                @pl.when(lead)
                def _():
                    go(gap_over(fm // per))

            root_send(fm, start)

        @pl.when(other_ok)
        def _():
            if start:
                wait_row(om)

                @pl.when(lead)
                def _():
                    wait_gap(om // per)
            root_send(om, start)

    def col_stage(n, start, p, dist, device):
        _, _, fm, flow_ok, om, other_ok = arrivals(n)
        for m, ok in ((fm, flow_ok), (om, other_ok)):
            @pl.when(ok)
            def _():
                if start:
                    wait_col(m, p)

                @pl.when((dist > 0) & (dist < nr - 1))
                def _():
                    copy = col_copy(m, p, device, False)
                    copy.start() if start else copy.wait_send()

    contract = (((1,), (1,)), ((), ()))

    def factors(b, t):
        moment = jnp.where(t == 0, 0.25, jnp.where(t == 1, 0.5, jnp.where(t == 2, 1.0, 2.0))).astype(jnp.float32)
        return jnp.exp(-gaps[b].astype(jnp.float32) * moment)

    def product(k, scale, low, size):
        panel = (rows[k, :, pl.ds(low, size)].astype(jnp.float32) * scale[:, low:low + size]).astype(jnp.bfloat16)
        return lax.dot_general(panel, cols[k, :, pl.ds(low, size)], contract, preferred_element_type=jnp.float32)

    def occ_green(k, scale):
        return product(k, scale, 0, nocc)

    def virt_green(k, scale):
        return product(k, scale, nocc, nall - nocc)

    def add(t, ks, base, held, occ_at, virt_at):
        slots = []
        for k in ks:
            for q in range(transfers):
                d = partner_ref[q, k] - base
                slots.append(jnp.minimum(jnp.where(d < 0, d + K, d), held - 1))

        def piece(p, inner):
            here = pl.ds(pl.multiple_of(p * SUB, SUB), SUB)
            sums = [chi[q, t, here, :] for q in range(transfers)]
            for a in range(len(ks)):
                occ = occ_at(a, here)
                for q in range(transfers):
                    sums[q] = sums[q] + occ * virt_at(slots[a * transfers + q], here)
            for q in range(transfers):
                chi[q, t, here, :] = sums[q]
            return inner

        lax.fori_loop(0, npts // SUB, piece, 0, unroll=2)

    def task(b, t):
        prev = (b + nk - 1) % nk
        for which, blk in ((0, prev), (1, b)):
            factor = factors(blk, t)
            for a in range(per):
                scale = factor[a:a + 1]
                vg[which * per + a] = virt_green(blk * per + a, scale)
                if which == 1:
                    og[a] = occ_green(blk * per + a, scale)
        add(t, [b * per + a for a in range(per)], prev * per, 2 * per,
            lambda a, here: og[a, here, :], lambda slot, here: vg[slot, here, :])

    hops = nr - 1
    total = nc * span
    edge = (c == 0) | (c == nc - 1)
    final = jnp.where(c == 0, nk - 2, 1)

    def prepare(t, inner):
        for first, blk in ((0, final - 1), (2 * per, final + 1)):
            factor = factors(blk, t)
            for a in range(per):
                scale = factor[a:a + 1]
                last_vg[t, first + a] = virt_green(blk * per + a, scale)
                if first > 0:
                    last_og[t, a] = occ_green(blk * per + a, scale)
        return inner

    def stream(a):
        m = final * per + a

        def one(t, inner):
            row = lax.broadcasted_iota(jnp.int32, (PAD, nall), 0)
            scale = jnp.sum(jnp.where(row == a, factors(final, t), 0.0), axis=0, keepdims=True)
            last_vg[t, per + a] = virt_green(m, scale)
            og[0] = occ_green(m, scale)
            add(t, [m], (final - 1) * per, 3 * per, lambda _, here: og[0, here, :], lambda slot, here: last_vg[t, slot, here, :])
            return inner

        lax.fori_loop(0, NTAU, one, 0)

    def close(t, inner):
        add(t, [(final + 1) * per + a for a in range(per)], (final - 1) * per, 3 * per,
            lambda a, here: last_og[t, a, here, :], lambda slot, here: last_vg[t, slot, here, :])
        return inner

    def work(n):
        v = n - hops - (span - 1)
        h, idx = v // span, v % span
        low, high = c - h, c + h
        rest = n - hops - (total - span + per - 1)

        @pl.when(edge & (rest == 0))
        def _():
            lax.fori_loop(0, NTAU, prepare, 0)

        @pl.when(edge & (rest > 0) & (rest <= per))
        def _():
            stream(rest - 1)

        @pl.when(edge & (rest == per))
        def _():
            lax.fori_loop(0, NTAU, close, 0)

        def one(w, inner):
            b_edge = jnp.where((h == 0) | (c > 0), 2 * low + 1 + w, 2 * high + w)
            ok_edge = (idx < NTAU) & ((h > 0) | (w == 0))
            b_mid = jnp.where(w == 0, 2 * low + 1 + idx % 2, 2 * high + idx % 2)
            ok_mid = jnp.where(w == 0, (low >= 0) & ((h > 0) | (idx % 2 == 0)), (high < nc) & (h > 0))
            ok = (v >= 0) & (h < nc - 1) & jnp.where(edge, ok_edge, ok_mid)
            wrap = w == 2
            ok = jnp.where(wrap, (rest >= 0) & (rest < NTAU), ok)
            b = jnp.where(wrap, 0, jnp.where(edge, b_edge, b_mid))
            t = jnp.where(wrap, rest, jnp.where(edge, idx, idx // 2))

            @pl.when(ok)
            def _():
                task(b, t)

            return inner

        lax.fori_loop(0, 3, one, 0)

    def clear(p, inner):
        q, t = p // NTAU, p % NTAU
        chi[q, t] = jnp.zeros((npts, ncol), jnp.float32)
        return inner

    def step(n, carry):
        @pl.when(n < total)
        def _():
            row_stage(n, True)

        @pl.when(n == 0)
        def _():
            lax.fori_loop(0, transfers * NTAU, clear, 0)

        for p, dist, device in ways:
            then = n - jnp.maximum(dist, 1)

            @pl.when((then >= 0) & (then < total))
            def _():
                col_stage(then, True, p, dist, device)

        work(n)
        return carry

    lax.fori_loop(0, total + hops, step, 0)

    def finish(n, carry):
        row_stage(n, False)
        for p, dist, device in ways:
            col_stage(n, False, p, dist, device)
        return carry

    lax.fori_loop(0, total, finish, 0)


def on_device(nk, nr, occ_orbitals, virt_orbitals, occ_gap, virt_gap, partner):
    per, npts, nocc = occ_orbitals.shape
    nv = virt_orbitals.shape[2]
    K, ncol, nall = nk * per, npts * nr // nk, nocc + nv
    transfers = partner.shape[0]
    gaps = jnp.pad(jnp.concatenate([occ_gap, virt_gap], axis=1), ((0, PAD - per), (0, 0)))
    dma = pltpu.SemaphoreType.DMA
    return pl.pallas_call(
        functools.partial(kernel, nk, nr, per),
        out_shape=jax.ShapeDtypeStruct((transfers, NTAU, npts, ncol), jnp.float32),
        in_specs=[pl.BlockSpec(memory_space=pl.ANY)] * 3 + [pl.BlockSpec(memory_space=pltpu.SMEM)],
        out_specs=pl.BlockSpec(memory_space=pltpu.VMEM),
        scratch_shapes=[
            pltpu.VMEM((K, npts, nall), jnp.bfloat16),
            pltpu.VMEM((K, ncol, nall), jnp.bfloat16),
            pltpu.VMEM((nk, PAD, nall), jnp.bfloat16),
            pltpu.VMEM((per, npts, ncol), jnp.float32),
            pltpu.VMEM((2 * per, npts, ncol), jnp.float32),
            pltpu.VMEM((NTAU, per, npts, ncol), jnp.float32),
            pltpu.VMEM((NTAU, 3 * per, npts, ncol), jnp.float32),
            dma((per, 2)), dma((K,)), dma((K,)), dma((K,)), dma((nk,)), dma((nk,)), dma((nk,)),
            dma((K, PIECES)), dma((K, PIECES)),
        ],
        compiler_params=pltpu.CompilerParams(
            collective_id=0, has_side_effects=True, vmem_limit_bytes=67043328),
    )(occ_orbitals, virt_orbitals, gaps, partner)


def solution(mesh):
    in_specs = (P("kpt", "row", None), P("kpt", "row", None), P("kpt", None), P("kpt", None), P())
    out_specs = P(None, None, "row", "kpt")
    return jax.shard_map(
        functools.partial(on_device, mesh.shape["kpt"], mesh.shape["row"]),
        mesh=mesh, in_specs=in_specs, out_specs=out_specs, check_vma=False,
    )
```

time: 172 us -> 144 us (0.84)
  Pallas kernels: 163 us -> 135 us
    pallas_call x1, Pallas kernels: 163 us -> 135 us  [on_device(): pl.pallas_call(functools.partial(kernel, nk, nr, per), out_shape=jax.Shap...]
where the time goes in v1:
time: 144 us; the launch traced here: 142 us
  Pallas kernels  135 us (94%)
  local copies, waits for them, and re-layouts  5.89 us (4%)
    pallas_call x1, Pallas kernels, on_device(): pl.pallas_call(functools.partial(kernel, nk, nr, per), out_shape=jax.Shap...  135 us
    unnamed x1, local copies, waits for them, and re-layouts  5.89 us

profile of v1, /device:TPU:2, one launch (start us, length us, event | category | flops | bytes accessed | tf_op | source)
XLA Modules:
  0.0 141.9 jit_solution(11165007468280673161)
XLA Ops:
  0.0 1.3 fusion.2.gap_ref
  1.3 134.7 %shard_map.55 = f32[3,4,512,256]{3,2,1,0:T(8,128)} custom-call(bf16[4,512,128]{2,1,0:T(8,128)(2,1)} %occ_ref.1, bf16[4,512,256]{2,1,0:T(8,128)(2,1)} %virt_ref.1, bf16[16,384]{1,0:T(8,128)(2,1)} %fusion.2.gap_ref, s32[3,32]{1,0:T(4,128)} %partner_ref.1), custom_call_target="tpu_custom_call" | custom-call | tf_op jit(solution)/shard_map/pallas_call | solution.py:363
  136.0 5.9 %copy.7 = f32[3,4,512,256]{3,2,1,0:T(8,128)} copy(f32[3,4,512,256]{3,2,1,0:T(8,128)} %shard_map.55) | data formatting | bytes 12582912

commit v2 on v1

--- a/solution.py
+++ b/solution.py
@@ -8,13 +8,13 @@
 from jax.sharding import PartitionSpec as P
 
 NTAU = 4
-PAD = 16
 SUB = 32
 PIECES = 4
-
-
-def kernel(nk, nr, per, occ_ref, virt_ref, gap_ref, partner_ref, chi, rows, cols, gaps, og, vg, last_og, last_vg,
-           local_sem, row_recv, flow_send, sib_send, gap_recv, gap_flow, gap_sib, col_recv, col_send):
+BEHIND = 12
+
+
+def kernel(nk, nr, per, occ_ref, virt_ref, occ_gap_ref, virt_gap_ref, partner_ref, chi, rows, cols, gaps, og, vg, last_og, last_vg,
+           local_sem, gap_sem, row_recv, flow_send, sib_send, gap_recv, gap_flow, gap_sib, col_recv, col_send):
     K = nk * per
     npts, nocc = occ_ref.shape[1], occ_ref.shape[2]
     nall = rows.shape[2]
@@ -52,8 +52,10 @@
         return (pltpu.make_async_copy(occ_ref.at[a], rows.at[m, :, pl.ds(0, nocc)], local_sem.at[a, 0]),
                 pltpu.make_async_copy(virt_ref.at[a], rows.at[m, :, pl.ds(nocc, nall - nocc)], local_sem.at[a, 1]))
 
-    local_gap = pltpu.make_async_copy(gap_ref, gaps.at[j], gap_recv.at[j])
-    local_gap.start()
+    local_gaps = (pltpu.make_async_copy(occ_gap_ref, gaps.at[j, :, pl.ds(0, nocc)], gap_sem.at[0]),
+                  pltpu.make_async_copy(virt_gap_ref, gaps.at[j, :, pl.ds(nocc, nall - nocc)], gap_sem.at[1]))
+    for copy in local_gaps:
+        copy.start()
     for a in range(per):
         for copy in local_rows(a):
             copy.start()
@@ -151,13 +153,18 @@
                     for copy in local_rows(idx % per):
                         copy.wait()
 
+                    @pl.when(lead)
+                    def _():
+                        for copy in local_gaps:
+                            copy.wait()
+
                 @pl.when(jnp.logical_not(own))
                 def _():
                     wait_row(fm)
 
-                @pl.when(lead)
-                def _():
-                    wait_gap(fm // per)
+                    @pl.when(lead)
+                    def _():
+                        wait_gap(fm // per)
 
             @pl.when(has_next)
             def _():
@@ -253,21 +260,23 @@
     edge = (c == 0) | (c == nc - 1)
     final = jnp.where(c == 0, nk - 2, 1)
 
-    def prepare(t, inner):
-        for first, blk in ((0, final - 1), (2 * per, final + 1)):
-            factor = factors(blk, t)
+    def prepare(t, after):
+        blk = jnp.where(after, final + 1, final - 1)
+        first = jnp.where(after, 2 * per, 0)
+        factor = factors(blk, t)
+        for a in range(per):
+            last_vg[t, first + a] = virt_green(blk * per + a, factor[a:a + 1])
+
+        @pl.when(after)
+        def _():
             for a in range(per):
-                scale = factor[a:a + 1]
-                last_vg[t, first + a] = virt_green(blk * per + a, scale)
-                if first > 0:
-                    last_og[t, a] = occ_green(blk * per + a, scale)
-        return inner
+                last_og[t, a] = occ_green(blk * per + a, factor[a:a + 1])
 
     def stream(a):
         m = final * per + a
 
         def one(t, inner):
-            row = lax.broadcasted_iota(jnp.int32, (PAD, nall), 0)
+            row = lax.broadcasted_iota(jnp.int32, (per, nall), 0)
             scale = jnp.sum(jnp.where(row == a, factors(final, t), 0.0), axis=0, keepdims=True)
             last_vg[t, per + a] = virt_green(m, scale)
             og[0] = occ_green(m, scale)
@@ -287,9 +296,15 @@
         low, high = c - h, c + h
         rest = n - hops - (total - span + per - 1)
 
-        @pl.when(edge & (rest == 0))
-        def _():
-            lax.fori_loop(0, NTAU, prepare, 0)
+        early = rest + span
+
+        def ready(t, inner):
+            prepare(jnp.where(rest == 0, t, early), jnp.where(rest == 0, c == 0, c > 0))
+            return inner
+
+        @pl.when(edge & ((rest == 0) | ((early >= 0) & (early < NTAU))))
+        def _():
+            lax.fori_loop(0, jnp.where(rest == 0, NTAU, 1), ready, 0)
 
         @pl.when(edge & (rest > 0) & (rest <= per))
         def _():
@@ -323,6 +338,11 @@
         chi[q, t] = jnp.zeros((npts, ncol), jnp.float32)
         return inner
 
+    def sent(n):
+        row_stage(n, False)
+        for p, dist, device in ways:
+            col_stage(n, False, p, dist, device)
+
     def step(n, carry):
         @pl.when(n < total)
         def _():
@@ -339,18 +359,20 @@
             def _():
                 col_stage(then, True, p, dist, device)
 
+        @pl.when((n >= BEHIND) & (n < total))
+        def _():
+            sent(n - BEHIND)
+
         work(n)
         return carry
 
     lax.fori_loop(0, total + hops, step, 0)
 
     def finish(n, carry):
-        row_stage(n, False)
-        for p, dist, device in ways:
-            col_stage(n, False, p, dist, device)
+        sent(n)
         return carry
 
-    lax.fori_loop(0, total, finish, 0)
+    lax.fori_loop(total - BEHIND, total, finish, 0)
 
 
 def on_device(nk, nr, occ_orbitals, virt_orbitals, occ_gap, virt_gap, partner):
@@ -358,27 +380,26 @@
     nv = virt_orbitals.shape[2]
     K, ncol, nall = nk * per, npts * nr // nk, nocc + nv
     transfers = partner.shape[0]
-    gaps = jnp.pad(jnp.concatenate([occ_gap, virt_gap], axis=1), ((0, PAD - per), (0, 0)))
     dma = pltpu.SemaphoreType.DMA
     return pl.pallas_call(
         functools.partial(kernel, nk, nr, per),
-        out_shape=jax.ShapeDtypeStruct((transfers, NTAU, npts, ncol), jnp.float32),
-        in_specs=[pl.BlockSpec(memory_space=pl.ANY)] * 3 + [pl.BlockSpec(memory_space=pltpu.SMEM)],
+        out_shape=pltpu.VMEM((transfers, NTAU, npts, ncol), jnp.float32),
+        in_specs=[pl.BlockSpec(memory_space=pl.ANY)] * 4 + [pl.BlockSpec(memory_space=pltpu.SMEM)],
         out_specs=pl.BlockSpec(memory_space=pltpu.VMEM),
         scratch_shapes=[
             pltpu.VMEM((K, npts, nall), jnp.bfloat16),
             pltpu.VMEM((K, ncol, nall), jnp.bfloat16),
-            pltpu.VMEM((nk, PAD, nall), jnp.bfloat16),
+            pltpu.VMEM((nk, per, nall), jnp.bfloat16),
             pltpu.VMEM((per, npts, ncol), jnp.float32),
             pltpu.VMEM((2 * per, npts, ncol), jnp.float32),
             pltpu.VMEM((NTAU, per, npts, ncol), jnp.float32),
             pltpu.VMEM((NTAU, 3 * per, npts, ncol), jnp.float32),
-            dma((per, 2)), dma((K,)), dma((K,)), dma((K,)), dma((nk,)), dma((nk,)), dma((nk,)),
+            dma((per, 2)), dma((2,)), dma((K,)), dma((K,)), dma((K,)), dma((nk,)), dma((nk,)), dma((nk,)),
             dma((K, PIECES)), dma((K, PIECES)),
         ],
         compiler_params=pltpu.CompilerParams(
-            collective_id=0, has_side_effects=True, vmem_limit_bytes=67043328),
-    )(occ_orbitals, virt_orbitals, gaps, partner)
+            collective_id=0, has_side_effects=True, vmem_limit_bytes=57 * 2**20),
+    )(occ_orbitals, virt_orbitals, occ_gap, virt_gap, partner)
 
 
 def solution(mesh):

time: 144 us -> 135 us (0.938)
  Pallas kernels: 135 us -> 130 us
  local copies, waits for them, and re-layouts: 5.89 us -> 2.71 us
    pallas_call x1, Pallas kernels: 135 us -> 130 us  [on_device(): pl.pallas_call(functools.partial(kernel, nk, nr, per), out_shape=pltpu.VM...]
    unnamed x1, local copies, waits for them, and re-layouts: 5.89 us -> 2.71 us
where the time goes in v2:
time: 135 us; the launch traced here: 132 us
  Pallas kernels  130 us (96%)
  local copies, waits for them, and re-layouts  2.71 us (2%)
    pallas_call x1, Pallas kernels, on_device(): pl.pallas_call(functools.partial(kernel, nk, nr, per), out_shape=pltpu.VM...  130 us
    unnamed x1, local copies, waits for them, and re-layouts  2.71 us

profile of v2, /device:TPU:2, one launch (start us, length us, event | category | flops | bytes accessed | tf_op | source)
XLA Modules:
  0.0 132.4 jit_solution(12971398029403604722)
XLA Ops:
  0.0 129.7 %shard_map.55 = f32[3,4,512,256]{3,2,1,0:T(8,128)S(1)} custom-call(bf16[4,512,128]{2,1,0:T(8,128)(2,1)} %occ_ref.1, bf16[4,512,256]{2,1,0:T(8,128)(2,1)} %virt_ref.1, bf16[4,128]{1,0:T(4,128)(2,1)} %occ_gap_ref.1, bf16[4,256]{1,0:T(4,128)(2,1)} %virt_gap_ref.1, s32[3,32]{1,0:T(4,128)} %partner_ref.1), custom_call_target="tpu_custom_call" | custom-call | tf_op jit(solution)/shard_map/pallas_call | solution.py:384
  129.7 2.7 %copy.7 = f32[3,4,512,256]{3,2,1,0:T(8,128)} copy(f32[3,4,512,256]{3,2,1,0:T(8,128)S(1)} %shard_map.55) | data formatting | bytes 12582912

commit v3 on v2

--- a/solution.py
+++ b/solution.py
@@ -129,18 +129,18 @@
                     root_copy(m, p).start()
 
     def arrivals(n):
-        h, idx = n // span, n % span
+        h, idx = lax.div(n, span), lax.rem(n, span)
         low, high = c - h, c + h
         first = low * span + idx
-        second = high * span + (idx + per) % span
+        second = high * span + lax.rem(idx + per, span)
         flow_ok = jnp.where(up, low >= 0, high < nc)
         other_ok = (h > 0) & jnp.where(up, high < nc, low >= 0)
         return h, idx, jnp.where(up, first, second), flow_ok, jnp.where(up, second, first), other_ok
 
-    def row_stage(n, start):
-        h, idx, fm, flow_ok, om, other_ok = arrivals(n)
+    def row_stage(came, start):
+        h, idx, fm, flow_ok, om, other_ok = came
         own = (h == 0) & (idx < per)
-        lead = idx % per == 0
+        lead = lax.rem(idx, per) == 0
 
         def go(copy):
             copy.start() if start else copy.wait_send()
@@ -150,7 +150,7 @@
             if start:
                 @pl.when(own)
                 def _():
-                    for copy in local_rows(idx % per):
+                    for copy in local_rows(lax.rem(idx, per)):
                         copy.wait()
 
                     @pl.when(lead)
@@ -164,7 +164,7 @@
 
                     @pl.when(lead)
                     def _():
-                        wait_gap(fm // per)
+                        wait_gap(lax.div(fm, per))
 
             @pl.when(has_next)
             def _():
@@ -172,7 +172,7 @@
 
                 @pl.when(lead)
                 def _():
-                    go(gap_on(fm // per))
+                    go(gap_on(lax.div(fm, per)))
 
             @pl.when((h > 0) | own)
             def _():
@@ -180,7 +180,7 @@
 
                 @pl.when(lead)
                 def _():
-                    go(gap_over(fm // per))
+                    go(gap_over(lax.div(fm, per)))
 
             root_send(fm, start)
 
@@ -191,11 +191,11 @@
 
                 @pl.when(lead)
                 def _():
-                    wait_gap(om // per)
+                    wait_gap(lax.div(om, per))
             root_send(om, start)
 
-    def col_stage(n, start, p, dist, device):
-        _, _, fm, flow_ok, om, other_ok = arrivals(n)
+    def col_stage(came, start, p, dist, device):
+        _, _, fm, flow_ok, om, other_ok = came
         for m, ok in ((fm, flow_ok), (om, other_ok)):
             @pl.when(ok)
             def _():
@@ -255,9 +255,10 @@
         add(t, [b * per + a for a in range(per)], prev * per, 2 * per,
             lambda a, here: og[a, here, :], lambda slot, here: vg[slot, here, :])
 
-    hops = nr - 1
     total = nc * span
     edge = (c == 0) | (c == nc - 1)
+    lag = jnp.where(edge, 1, 2)
+    hops = lag * jnp.maximum(jnp.maximum(dist_a, dist_b), 1)
     final = jnp.where(c == 0, nk - 2, 1)
 
     def prepare(t, after):
@@ -292,19 +293,21 @@
 
     def work(n):
         v = n - hops - (span - 1)
-        h, idx = v // span, v % span
+        h, idx = lax.div(jnp.maximum(v, 0), span), lax.rem(jnp.maximum(v, 0), span)
         low, high = c - h, c + h
         rest = n - hops - (total - span + per - 1)
 
         early = rest + span
+        at_once = (rest == 0) & (c > 0)
+        each = jnp.where(rest < 0, early, rest)
 
         def ready(t, inner):
-            prepare(jnp.where(rest == 0, t, early), jnp.where(rest == 0, c == 0, c > 0))
+            prepare(jnp.where(at_once, t, each), jnp.where(rest < 0, c > 0, c == 0))
             return inner
 
-        @pl.when(edge & ((rest == 0) | ((early >= 0) & (early < NTAU))))
-        def _():
-            lax.fori_loop(0, jnp.where(rest == 0, NTAU, 1), ready, 0)
+        @pl.when(edge & (at_once | ((each >= 0) & (each < NTAU) & ((rest < 0) | (c == 0)))))
+        def _():
+            lax.fori_loop(0, jnp.where(at_once, NTAU, 1), ready, 0)
 
         @pl.when(edge & (rest > 0) & (rest <= per))
         def _():
@@ -339,25 +342,28 @@
         return inner
 
     def sent(n):
-        row_stage(n, False)
+        came = arrivals(n)
+        row_stage(came, False)
         for p, dist, device in ways:
-            col_stage(n, False, p, dist, device)
+            col_stage(came, False, p, dist, device)
 
     def step(n, carry):
         @pl.when(n < total)
         def _():
-            row_stage(n, True)
+            row_stage(arrivals(n), True)
 
         @pl.when(n == 0)
         def _():
             lax.fori_loop(0, transfers * NTAU, clear, 0)
 
+        thens = [n - lag * jnp.maximum(dist, 1) for dist in (dist_a, dist_b)]
+        cames = [arrivals(jnp.maximum(then, 0)) for then in thens]
         for p, dist, device in ways:
-            then = n - jnp.maximum(dist, 1)
+            then = thens[p % 2]
 
             @pl.when((then >= 0) & (then < total))
             def _():
-                col_stage(then, True, p, dist, device)
+                col_stage(cames[p % 2], True, p, dist, device)
 
         @pl.when((n >= BEHIND) & (n < total))
         def _():

time: 135 us -> 134 us (level); the launches traced: 132 us -> 134 us
    pallas_call x1, Pallas kernels: 130 us -> 131 us  [on_device(): pl.pallas_call(functools.partial(kernel, nk, nr, per), out_shape=pltpu.VM...]
where the time goes in v3:
time: 134 us
  Pallas kernels  131 us (98%)
  local copies, waits for them, and re-layouts  2.71 us (2%)
    pallas_call x1, Pallas kernels, on_device(): pl.pallas_call(functools.partial(kernel, nk, nr, per), out_shape=pltpu.VM...  131 us
    unnamed x1, local copies, waits for them, and re-layouts  2.71 us

profile of v3, /device:TPU:2, one launch (start us, length us, event | category | flops | bytes accessed | tf_op | source)
XLA Modules:
  0.0 133.8 jit_solution(15899232598686556353)
XLA Ops:
  0.0 131.1 %shard_map.55 = f32[3,4,512,256]{3,2,1,0:T(8,128)S(1)} custom-call(bf16[4,512,128]{2,1,0:T(8,128)(2,1)} %occ_ref.1, bf16[4,512,256]{2,1,0:T(8,128)(2,1)} %virt_ref.1, bf16[4,128]{1,0:T(4,128)(2,1)} %occ_gap_ref.1, bf16[4,256]{1,0:T(4,128)(2,1)} %virt_gap_ref.1, s32[3,32]{1,0:T(4,128)} %partner_ref.1), custom_call_target="tpu_custom_call" | custom-call | tf_op jit(solution)/shard_map/pallas_call | solution.py:390
  131.1 2.7 %copy.7 = f32[3,4,512,256]{3,2,1,0:T(8,128)} copy(f32[3,4,512,256]{3,2,1,0:T(8,128)S(1)} %shard_map.55) | data formatting | bytes 12582912

commit v4 on v3

--- a/solution.py
+++ b/solution.py
@@ -323,10 +323,11 @@
             b_mid = jnp.where(w == 0, 2 * low + 1 + idx % 2, 2 * high + idx % 2)
             ok_mid = jnp.where(w == 0, (low >= 0) & ((h > 0) | (idx % 2 == 0)), (high < nc) & (h > 0))
             ok = (v >= 0) & (h < nc - 1) & jnp.where(edge, ok_edge, ok_mid)
-            wrap = w == 2
-            ok = jnp.where(wrap, (rest >= 0) & (rest < NTAU), ok)
+            wrap = w >= 2
+            turn = jnp.where(w == 3, 1, jnp.where(rest > 0, rest + 1, 0))
+            ok = jnp.where(wrap, (rest >= 0) & (turn < NTAU) & ((w == 2) | (rest == 0)), ok)
             b = jnp.where(wrap, 0, jnp.where(edge, b_edge, b_mid))
-            t = jnp.where(wrap, rest, jnp.where(edge, idx, idx // 2))
+            t = jnp.where(wrap, turn, jnp.where(edge, idx, idx // 2))
 
             @pl.when(ok)
             def _():
@@ -334,7 +335,7 @@
 
             return inner
 
-        lax.fori_loop(0, 3, one, 0)
+        lax.fori_loop(0, 4, one, 0)
 
     def clear(p, inner):
         q, t = p // NTAU, p % NTAU

time: 134 us -> 133 us (level)
  no operation moved by 1% of the time
where the time goes in v4:
time: 133 us
  Pallas kernels  130 us (98%)
  local copies, waits for them, and re-layouts  2.71 us (2%)
    pallas_call x1, Pallas kernels, on_device(): pl.pallas_call(functools.partial(kernel, nk, nr, per), out_shape=pltpu.VM...  130 us
    unnamed x1, local copies, waits for them, and re-layouts  2.71 us

profile of v4, /device:TPU:2, one launch (start us, length us, event | category | flops | bytes accessed | tf_op | source)
XLA Modules:
  0.0 133.0 jit_solution(3992524477083156556)
XLA Ops:
  0.0 130.2 %shard_map.55 = f32[3,4,512,256]{3,2,1,0:T(8,128)S(1)} custom-call(bf16[4,512,128]{2,1,0:T(8,128)(2,1)} %occ_ref.1, bf16[4,512,256]{2,1,0:T(8,128)(2,1)} %virt_ref.1, bf16[4,128]{1,0:T(4,128)(2,1)} %occ_gap_ref.1, bf16[4,256]{1,0:T(4,128)(2,1)} %virt_gap_ref.1, s32[3,32]{1,0:T(4,128)} %partner_ref.1), custom_call_target="tpu_custom_call" | custom-call | tf_op jit(solution)/shard_map/pallas_call | solution.py:391
  130.2 2.7 %copy.7 = f32[3,4,512,256]{3,2,1,0:T(8,128)} copy(f32[3,4,512,256]{3,2,1,0:T(8,128)S(1)} %shard_map.55) | data formatting | bytes 12582912
